TPU v7x, 256 devices: a whole 4x4x8 slice. The times are simulated.
256 devices in a mesh: group: 16 (over x_lo, z), shard: 16 (over x_hi, y, core).
Axes of the slice: x: 4 (x_hi: 2, x_lo: 2; x = x_hi * 2 + x_lo), y: 4, z: 8, core: 2. Of those that a mesh axis runs over, the one named last changes fastest.
Arguments:
- queries: bfloat16 [2, 3, 32768, 512], P(None, None, ('group', 'shard')), may hold values from -6 to 6
- key_tokens: bfloat16 [2, 3, 32768, 512], P(None, None, ('group', 'shard')), may hold values from -24 to 24
- value_tokens: bfloat16 [2, 3, 32768, 512], P(None, None, ('group', 'shard')), may hold values from -24 to 24
- token_rate: float32 [2, 3, 32768], P(None, None, ('group', 'shard')), may hold values from 0.1 to 1
- state_in: float32 [16, 3, 512, 3, 512], P('group', None, 'shard'), may hold values from -0.25 to 0.25
- init_state: float32 [3, 512, 3, 512], P(None, 'shard'), may hold values from -0.25 to 0.25
- norm_gain: float32 [3, 512], replicated, may hold values from 0.25 to 2.5
Outputs:
- head_output: bfloat16 [2, 3, 32768, 512], P(None, None, ('group', 'shard'))
- state_out: float32 [16, 3, 512, 3, 512], P('group', None, 'shard')
All inputs are finite; a program needn't handle non-finite values.
Results may differ from a plain program's by a relative error of at most 0.011.
Values may be sent and summed in bfloat16 or wider, within the bound.
A program may use at most 128 MiB of HBM per device.

v0:
```python
import jax
import jax.numpy as jnp
from jax import lax
from jax.sharding import PartitionSpec as P

epsilon = 1e-06


def shifted(value, axis, steps):
    count = lax.axis_size(axis)
    leading, last = (max(0, -steps), min(count, count - steps))
    return lax.ppermute(value, axis, [(source, source + steps) for source in range(leading, last)])


def forward(rows, packed):
    pre_gate = jnp.dot(rows, packed[:, 0], preferred_element_type=jnp.float32)
    pre_up = jnp.dot(rows, packed[:, 1], preferred_element_type=jnp.float32)
    sigmoid_gate = jax.nn.sigmoid(pre_gate)
    hidden = (pre_gate * sigmoid_gate * pre_up).astype(jnp.bfloat16)
    produced = lax.dot_general(
        hidden, packed[:, 2], (((1,), (1,)), ((), ())), preferred_element_type=jnp.float32
    )
    return (pre_gate, pre_up, sigmoid_gate, hidden, produced)


def on_device(queries, key_tokens, value_tokens, token_rate, state_in, init_state, norm_gain):
    head_count = queries.shape[1]
    token_rows = queries.shape[2]
    span = token_rows * lax.axis_size("shard")

    def head_pass(slot_index, head_index, packed, shard_weights):
        query_rows = queries[slot_index, head_index]
        key_rows = key_tokens[slot_index, head_index]
        value_rows = value_tokens[slot_index, head_index]
        rate_row = token_rate[slot_index, head_index]
        applied = forward(query_rows, packed)[4]
        normed = (
            applied
            * lax.rsqrt(jnp.mean(applied * applied, axis=-1, keepdims=True) + epsilon)
            * norm_gain[head_index]
        )
        pre_gate, pre_up, sigmoid_gate, hidden, guess = forward(key_rows, packed)
        error = (rate_row[:, None] * (guess - value_rows.astype(jnp.float32))).astype(jnp.bfloat16)
        back_hidden = jnp.dot(error, packed[:, 2], preferred_element_type=jnp.float32)
        grad_gate = (
            back_hidden * pre_up * sigmoid_gate * (1.0 + pre_gate * (1.0 - sigmoid_gate))
        ).astype(jnp.bfloat16)
        grad_up = (back_hidden * pre_gate * sigmoid_gate).astype(jnp.bfloat16)
        contract = (((0,), (0,)), ((), ()))
        gate_part = lax.dot_general(
            key_rows, grad_gate, contract, preferred_element_type=jnp.float32
        )
        up_part = lax.dot_general(key_rows, grad_up, contract, preferred_element_type=jnp.float32)
        down_part = lax.dot_general(error, hidden, contract, preferred_element_type=jnp.float32)
        summed = lax.psum_scatter(
            jnp.stack([gate_part, up_part, down_part], axis=1),
            "shard",
            scatter_dimension=0,
            tiled=True,
        )
        updated = shard_weights - summed / float(span)
        return (normed.astype(jnp.bfloat16), updated)

    def slot_pass(slot_index, shards):
        outputs = []
        updates = []
        arrivals = []
        for head_index in range(head_count):
            packed = lax.all_gather(
                shards[head_index].astype(jnp.bfloat16), "shard", axis=0, tiled=True
            )
            normed, updated = head_pass(slot_index, head_index, packed, shards[head_index])
            outputs.append(normed)
            updates.append(updated)
        return (outputs, updates, arrivals)

    first_outputs, middle, arrivals = slot_pass(0, state_in[0])
    arrived = shifted(jnp.stack(middle, axis=0).astype(jnp.bfloat16), "group", 1).astype(
        jnp.float32
    )
    arrived = jnp.where(lax.axis_index("group") == 0, init_state, arrived)
    second_outputs, final, unused = slot_pass(1, arrived)
    head_output = jnp.stack(
        [jnp.stack(first_outputs, axis=0), jnp.stack(second_outputs, axis=0)], axis=0
    )
    state_out = jnp.stack(final, axis=0)[None]
    return (head_output, state_out)


def solution(mesh):
    in_specs = (
        P(None, None, ("group", "shard"), None),
        P(None, None, ("group", "shard"), None),
        P(None, None, ("group", "shard"), None),
        P(None, None, ("group", "shard")),
        P("group", None, "shard", None, None),
        P(None, "shard", None, None),
        P(),
    )
    out_specs = (P(None, None, ("group", "shard"), None), P("group", None, "shard", None, None))
    return jax.shard_map(
        on_device, mesh=mesh, in_specs=in_specs, out_specs=out_specs, check_vma=False
    )
```

profile of v0, /device:TPU:32, one launch (start us, length us, event | category | flops | bytes accessed | tf_op | source)
XLA Modules:
  0.0 756.1 jit_solution(18101220173649434521)
XLA Ops:
  7.2 1.9 bitcast_convert_fusion.2
  11.4 53.0 %all-gather.9.cloned.1.call-done = bf16[512,3,512]{2,0,1:T(8,128)(2,1)} async-done(((bf16[32,3,512]{2,0,1:T(8,128)(2,1)}), bf16[512,3,512]{2,0,1:T(8,128)(2,1)}) %all-gather.9.cloned.1.call-update) | async-done | bytes 1572880 | tf_op jit(solution)/shard_map/all_gather | solution.py:69
  64.5 1.4 fusion.30
  68.4 1.3 convolution_bitcast_fusion.12
  69.7 48.0 %all-gather.11.cloned.1.call-done = bf16[512,3,512]{2,0,1:T(8,128)(2,1)} async-done(((bf16[32,3,512]{2,0,1:T(8,128)(2,1)}), bf16[512,3,512]{2,0,1:T(8,128)(2,1)}) %all-gather.11.cloned.1.call-update) | async-done | bytes 1572880 | tf_op jit(solution)/shard_map/all_gather | solution.py:69
  117.8 1.4 fusion.33
  119.2 1.3 multiply_convert_fusion.14
  121.7 1.3 convolution_bitcast_fusion.9
  123.2 1.3 convolution_bitcast_fusion.13
  124.8 1.3 convolution_bitcast_fusion.10
  126.1 1.3 convolution_bitcast_fusion.14
  127.5 1.3 convolution_bitcast_fusion.11
  128.8 42.3 %all-gather.7.cloned.1.call-done = bf16[512,3,512]{2,0,1:T(8,128)(2,1)} async-done(((bf16[32,3,512]{2,0,1:T(8,128)(2,1)}), bf16[512,3,512]{2,0,1:T(8,128)(2,1)}) %all-gather.7.cloned.1.call-update) | async-done | bytes 1572880 | tf_op jit(solution)/shard_map/all_gather | solution.py:69
  171.1 1.4 fusion.27
  176.6 3.5 copy.30
  180.1 2.2 pad_maximum_fusion.2
  182.3 3.6 copy.36
  185.8 2.2 pad_maximum_fusion.1
  188.0 3.6 copy.33
  193.5 179.7 %all-reduce.13.cloned.1.call-done = (f32[512,3,512]{2,1,0:T(4,128)}, f32[512,3,512]{2,1,0:T(4,128)}, f32[512,3,512]{2,1,0:T(4,128)}) async-done(((f32[512,3,512]{2,1,0:T(4,128)}, f32[512,3,512]{2,1,0:T(4,128)}, f32[512,3,512]{2,1,0:T(4,128)}), (f32[512,3,512]{2,1,0:T(4,128)}, f32[512,3,512]{2,1,0:T(4,128)}, f32[512,3,512]{2,1,0:T(4,128)})) %all-reduce.13.cloned.1.call-update) | async-done | bytes 9437200
  375.7 3.6 collective-permute-start
  379.3 5.1 collective-permute-done
  387.6 49.3 %all-gather.15.cloned.1.call-done = bf16[512,3,512]{2,0,1:T(8,128)(2,1)} async-done(((bf16[32,3,512]{2,0,1:T(8,128)(2,1)}), bf16[512,3,512]{2,0,1:T(8,128)(2,1)}) %all-gather.15.cloned.1.call-update) | async-done | bytes 1572880 | tf_op jit(solution)/shard_map/all_gather | solution.py:69
  437.0 1.4 convolution_bitcast_fusion.21
  438.4 1.3 multiply_convert_fusion.5
  440.9 1.3 convolution_bitcast_fusion.3
  442.2 47.4 %all-gather.17.cloned.1.call-done = bf16[512,3,512]{2,0,1:T(8,128)(2,1)} async-done(((bf16[32,3,512]{2,0,1:T(8,128)(2,1)}), bf16[512,3,512]{2,0,1:T(8,128)(2,1)}) %all-gather.17.cloned.1.call-update) | async-done | bytes 1572880 | tf_op jit(solution)/shard_map/all_gather | solution.py:69
  489.6 1.4 convolution_bitcast_fusion.19
  490.9 1.3 multiply_convert_fusion.2
  493.5 1.3 convolution_bitcast_fusion
  495.0 1.3 convolution_bitcast_fusion.4
  496.6 1.3 convolution_bitcast_fusion.1
  497.9 1.3 convolution_bitcast_fusion.5
  499.2 1.3 convolution_bitcast_fusion.2
  500.6 42.3 %all-gather.13.cloned.1.call-done = bf16[512,3,512]{2,0,1:T(8,128)(2,1)} async-done(((bf16[32,3,512]{2,0,1:T(8,128)(2,1)}), bf16[512,3,512]{2,0,1:T(8,128)(2,1)}) %all-gather.13.cloned.1.call-update) | async-done | bytes 1572880 | tf_op jit(solution)/shard_map/all_gather | solution.py:69
  542.9 1.4 convolution_bitcast_fusion.23
  548.4 3.5 copy.44
  551.9 2.2 pad_maximum_fusion.5
  554.0 3.6 copy.54
  557.6 2.2 pad_maximum_fusion.4
  559.8 3.6 copy.49
  565.9 2.2 multiply_reduce_fusion.4
  569.2 2.2 multiply_reduce_fusion.3
  572.6 2.2 multiply_reduce_fusion.5
  575.9 2.2 multiply_reduce_fusion.1
  579.3 2.2 multiply_reduce_fusion
  582.7 1.5 multiply_reduce_fusion.2
  585.7 159.4 %all-reduce.11.cloned.1.call-done = (f32[512,3,512]{2,1,0:T(4,128)}, f32[512,3,512]{2,1,0:T(4,128)}, f32[512,3,512]{2,1,0:T(4,128)}) async-done(((f32[512,3,512]{2,1,0:T(4,128)}, f32[512,3,512]{2,1,0:T(4,128)}, f32[512,3,512]{2,1,0:T(4,128)}), (f32[512,3,512]{2,1,0:T(4,128)}, f32[512,3,512]{2,1,0:T(4,128)}, f32[512,3,512]{2,1,0:T(4,128)})) %all-reduce.11.cloned.1.call-update) | async-done | bytes 9437200
  (121 shorter events, 38.2 us)
Async XLA Ops:
  7.2 58.8 %copy-start = (bf16[2,3,128,512]{3,2,1,0:T(8,128)(2,1)S(1)}, bf16[2,3,128,512]{3,2,1,0:T(8,128)(2,1)}, u32[]{:S(2)}) copy-start(bf16[2,3,128,512]{3,2,1,0:T(8,128)(2,1)} %param.8) | copy-start | bytes 2359300
  7.2 57.3 %all-gather.9.cloned.1.call-start = ((), (), s32[]{:S(2)}) async-start(), calls=%async_computation.1 | async-start | bytes 1671168 | tf_op jit(solution)/shard_map/all_gather | solution.py:69
  9.1 108.6 %all-gather.11.cloned.1.call-start = ((), (), s32[]{:S(2)}) async-start(), calls=%async_computation.2 | async-start | bytes 1671168 | tf_op jit(solution)/shard_map/all_gather | solution.py:69
  9.9 161.2 %all-gather.7.cloned.1.call-start = ((), (), s32[]{:S(2)}) async-start(), calls=%async_computation | async-start | bytes 1671168 | tf_op jit(solution)/shard_map/all_gather | solution.py:69
  10.6 362.5 %all-reduce.13.cloned.1.call-start = ((), (), s32[]{:S(2)}) async-start(), calls=%async_computation.7 | async-start | bytes 25165824
  64.5 2.7 copy-start.4
  117.8 2.7 copy-start.6
  171.1 2.7 copy-start.8
  191.6 0.7 copy-start.24
  191.6 183.8 %copy-start.16 = (f32[1,3,32,3,512]{4,2,3,1,0:T(8,128)S(1)}, f32[1,3,32,3,512]{4,2,3,1,0:T(8,128)}, u32[]{:S(2)}) copy-start(f32[1,3,32,3,512]{4,2,3,1,0:T(8,128)} %param.11) | copy-start | bytes 1769476
  191.6 245.4 %all-gather.15.cloned.1.call-start = ((), (), s32[]{:S(2)}) async-start(), calls=%async_computation.4 | async-start | bytes 1671168 | tf_op jit(solution)/shard_map/all_gather | solution.py:69
  374.1 10.3 %copy-start.17 = (f32[3,32,3,512]{3,1,2,0:T(8,128)S(1)}, f32[3,32,3,512]{3,1,2,0:T(8,128)}, u32[]{:S(2)}) copy-start(f32[3,32,3,512]{3,1,2,0:T(8,128)} %param.12) | copy-start | bytes 1769476
  375.6 61.4 %copy-start.1 = (bf16[2,3,128,512]{3,2,1,0:T(8,128)(2,1)S(1)}, bf16[2,3,128,512]{3,2,1,0:T(8,128)(2,1)}, u32[]{:S(2)}) copy-start(bf16[2,3,128,512]{3,2,1,0:T(8,128)(2,1)} %param.8) | copy-start | bytes 2359300
  375.7 8.7 %collective-permute-start = (bf16[3,32,3,512]{3,1,2,0:T(8,128)(2,1)S(1)}, bf16[3,32,3,512]{3,1,2,0:T(8,128)(2,1)S(1)}, u32[]{:S(2)}, u32[]{:S(2)}) collective-permute-start(bf16[3,32,3,512]{3,1,2,0:T(8,128)(2,1)S(1)} %pad_maximum_fusion.7), channel_id=1, source_target_pairs={{0,16},{16,32},{32,48},{48,64},{64,80},{80,96},{96,112},{112,128},... | collective-permute-start | bytes 884744 | tf_op jit(solution)/shard_map/ppermute | solution.py:12
  384.5 0.8 copy-start.2
  386.1 103.5 %all-gather.17.cloned.1.call-start = ((), (), s32[]{:S(2)}) async-start(), calls=%async_computation.5 | async-start | bytes 1671168 | tf_op jit(solution)/shard_map/all_gather | solution.py:69
  386.7 156.2 %all-gather.13.cloned.1.call-start = ((), (), s32[]{:S(2)}) async-start(), calls=%async_computation.3 | async-start | bytes 1671168 | tf_op jit(solution)/shard_map/all_gather | solution.py:69
  387.4 357.7 %all-reduce.11.cloned.1.call-start = ((), (), s32[]{:S(2)}) async-start(), calls=%async_computation.6 | async-start | bytes 25165824
  437.0 2.7 copy-start.10
  489.6 2.7 copy-start.12
  542.9 2.7 copy-start.14
  563.3 0.7 copy-start.23
  563.3 1.4 copy-start.5
  565.9 2.2 copy-start.7
  569.2 2.2 copy-start.9
  572.6 2.2 copy-start.11
  575.9 2.2 copy-start.13
  579.3 2.2 copy-start.15
  582.6 1.6 copy-start.20
  582.6 1.6 copy-start.22
  582.6 1.7 copy-start.19
  582.7 1.7 copy-start.21
  582.7 1.8 copy-start.18
  584.7 163.4 %copy-start.3 = (f32[3,32,3,512]{3,1,2,0:T(8,128)S(1)}, f32[3,32,3,512]{3,1,2,0:T(8,128)}, u32[]{:S(2)}) copy-start(f32[3,32,3,512]{3,1,2,0:T(8,128)} %copy-done.2) | copy-start | bytes 1769476
Sparse Core Ops, SparseCore 0:
  10.8 53.6 all-gather.8
  67.8 49.8 all-gather.10
  121.2 49.8 all-gather.6
  191.7 181.3 all-reduce.12
  386.2 50.7 all-gather.14
  439.6 49.8 all-gather.16
  492.9 49.8 all-gather.12
  563.5 181.5 all-reduce.10
where the time goes:
time: 757 us; the launch traced here: 756 us
  waiting for transfers between devices  629 us (83%)
  matrix products  61.9 us (8%)
  local copies, waits for them, and re-layouts  33.3 us (4%)
  between operations  15.4 us (2%)
  other arithmetic  12.2 us (2%)
    unnamed x10, waiting for transfers between devices  342 us
    all_gather x6, waiting for transfers between devices, slot_pass(): lax.all_gather(shards[head_index].astype(jnp.bfloat16), 'shard', axis=0,...  282 us
    another operation x6, local copies, waits for them, and re-layouts, head_pass(): jnp.stack([gate_part, up_part, down_part], axis=1)  21.3 us
    dot_general x12, matrix products, forward(): lax.dot_general(hidden, packed[:, 2], (((1,), (1,)), ((), ())), preferred...  19.7 us
    dot_general x12, matrix products, forward(): pre_gate = jnp.dot(rows, packed[:, 0], preferred_element_type=jnp.float32)  15.2 us
  transfers between devices with their start and end apart: 9, of which 9 were waited for; matrix products, arithmetic and copies ran while one was open for 7% of the time, Pallas kernels for 0%

commit v1 on v0

--- a/solution.py
+++ b/solution.py
@@ -66,8 +66,14 @@
         updates = []
         arrivals = []
         for head_index in range(head_count):
-            packed = lax.all_gather(
-                shards[head_index].astype(jnp.bfloat16), "shard", axis=0, tiled=True
+            packed = jnp.concatenate(
+                lax.all_to_all(
+                    jnp.stack([shards[head_index].astype(jnp.bfloat16)] * lax.axis_size("shard")),
+                    "shard",
+                    0,
+                    0,
+                ),
+                axis=0,
             )
             normed, updated = head_pass(slot_index, head_index, packed, shards[head_index])
             outputs.append(normed)

time: 757 us -> 627 us (0.83)
  waiting for transfers between devices: 629 us -> 463 us
  starting transfers between devices: 4.09 us -> 32.4 us
  local copies, waits for them, and re-layouts: 33.3 us -> 46.9 us
    all_gather x6 -> x0, waiting for transfers between devices: 282 us -> none  [slot_pass(): lax.all_gather(shards[head_index].astype(jnp.bfloat16), 'shard', axis=0,...]
    all_to_all x0 -> x6, waiting for transfers between devices: none -> 117 us  [slot_pass(): lax.all_to_all(jnp.stack([shards[head_index].astype(jnp.bfloat16)] * lax....]
    all_to_all x0 -> x6, starting transfers between devices: none -> 28.6 us  [slot_pass(): lax.all_to_all(jnp.stack([shards[head_index].astype(jnp.bfloat16)] * lax....]
    all_to_all x0 -> x6, local copies, waits for them, and re-layouts: none -> 9.21 us  [slot_pass(): lax.all_to_all(jnp.stack([shards[head_index].astype(jnp.bfloat16)] * lax....]
    another operation x0 -> x16, local copies, waits for them, and re-layouts: none -> 8.89 us  [the longest x10 8.61 us: slot_pass(): jnp.stack([shards[head_index].astype(jnp.bfloat16)] * lax.axis_size('shar...]
    unnamed x10 -> x4, waiting for transfers between devices: 342 us -> 340 us
where the time goes in v1:
time: 627 us; the launch traced here: 626 us
  waiting for transfers between devices  463 us (74%)
  matrix products  58.7 us (9%)
  local copies, waits for them, and re-layouts  46.9 us (7%)
  starting transfers between devices  32.4 us (5%)
  between operations  15.7 us (3%)
  other arithmetic  9.46 us (2%)
    unnamed x4, waiting for transfers between devices  340 us
    all_to_all x6, waiting for transfers between devices, slot_pass(): lax.all_to_all(jnp.stack([shards[head_index].astype(jnp.bfloat16)] * lax....  117 us
    all_to_all x6, starting transfers between devices, slot_pass(): lax.all_to_all(jnp.stack([shards[head_index].astype(jnp.bfloat16)] * lax....  28.6 us
    another operation x6, local copies, waits for them, and re-layouts, head_pass(): jnp.stack([gate_part, up_part, down_part], axis=1)  21.4 us
    dot_general x12, matrix products, forward(): lax.dot_general(hidden, packed[:, 2], (((1,), (1,)), ((), ())), preferred...  19.6 us
  transfers between devices with their start and end apart: 9, of which 9 were waited for; matrix products, arithmetic and copies ran while one was open for 7% of the time, Pallas kernels for 0%

profile of v1, /device:TPU:32, one launch (start us, length us, event | category | flops | bytes accessed | tf_op | source)
XLA Modules:
  0.0 625.8 jit_solution(18220433987506013607)
XLA Ops:
  9.3 1.4 stack.110
  10.7 7.0 %all-to-all-start.1 = ((bf16[16,32,3,512]{3,1,2,0:T(8,128)(2,1)}), bf16[16,32,3,512]{3,1,2,0:T(8,128)(2,1)S(1)}, u32[]{:S(2)}, u32[]{:S(2)}) async-start(bf16[16,32,3,512]{3,1,2,0:T(8,128)(2,1)} %stack.110), calls=%async_computation.1 | async-start | bytes 3145728 | tf_op jit(solution)/shard_map/all_to_all | solution.py:70
  17.8 23.6 %all-to-all-done.1 = bf16[16,32,3,512]{3,1,2,0:T(8,128)(2,1)S(1)} async-done(((bf16[16,32,3,512]{3,1,2,0:T(8,128)(2,1)}), bf16[16,32,3,512]{3,1,2,0:T(8,128)(2,1)S(1)}, u32[]{:S(2)}, u32[]{:S(2)}) %all-to-all-start.1) | async-done | bytes 1572896 | tf_op jit(solution)/shard_map/all_to_all | solution.py:70
  41.4 1.5 stack.112
  43.0 4.4 all-to-all-start.2
  47.7 1.6 copy.66
  51.8 19.4 %all-to-all-done.2 = bf16[16,32,3,512]{3,1,2,0:T(8,128)(2,1)} async-done(((bf16[16,32,3,512]{3,1,2,0:T(8,128)(2,1)}), bf16[16,32,3,512]{3,1,2,0:T(8,128)(2,1)}, u32[]{:S(2)}, u32[]{:S(2)}) %all-to-all-start.2) | async-done | bytes 1572896 | tf_op jit(solution)/shard_map/all_to_all | solution.py:70
  71.1 1.4 stack.108
  72.5 4.4 all-to-all-start
  77.0 1.5 copy.69
  78.5 1.5 convolution_bitcast_fusion.12
  82.4 1.3 convolution_bitcast_fusion.9
  85.0 15.6 %all-to-all-done = bf16[16,32,3,512]{3,1,2,0:T(8,128)(2,1)} async-done(((bf16[16,32,3,512]{3,1,2,0:T(8,128)(2,1)}), bf16[16,32,3,512]{3,1,2,0:T(8,128)(2,1)}, u32[]{:S(2)}, u32[]{:S(2)}) %all-to-all-start) | async-done | bytes 1572896 | tf_op jit(solution)/shard_map/all_to_all | solution.py:70
  100.6 1.5 copy.63
  108.4 3.5 copy.73
  112.0 1.4 convolution_bitcast_fusion.10
  115.0 3.6 copy.75
  118.6 1.4 convolution_bitcast_fusion.16
  121.7 3.6 copy.71
  127.2 180.4 %all-reduce.13.cloned.1.call-done = (f32[512,3,512]{2,1,0:T(4,128)}, f32[512,3,512]{2,1,0:T(4,128)}, f32[512,3,512]{2,1,0:T(4,128)}) async-done(((f32[512,3,512]{2,1,0:T(4,128)}, f32[512,3,512]{2,1,0:T(4,128)}, f32[512,3,512]{2,1,0:T(4,128)}), (f32[512,3,512]{2,1,0:T(4,128)}, f32[512,3,512]{2,1,0:T(4,128)}, f32[512,3,512]{2,1,0:T(4,128)})) %all-reduce.13.cloned.1.call-update) | async-done | bytes 9437200
  311.1 3.5 collective-permute-start
  314.6 5.1 collective-permute-done
  321.3 1.4 stack.136
  322.7 4.0 all-to-all-start.4
  326.7 23.6 %all-to-all-done.4 = bf16[16,32,3,512]{3,1,2,0:T(8,128)(2,1)S(1)} async-done(((bf16[16,32,3,512]{3,1,2,0:T(8,128)(2,1)}), bf16[16,32,3,512]{3,1,2,0:T(8,128)(2,1)S(1)}, u32[]{:S(2)}, u32[]{:S(2)}) %all-to-all-start.4) | async-done | bytes 1572896 | tf_op jit(solution)/shard_map/all_to_all | solution.py:70
  350.3 1.5 stack.139
  352.0 4.4 all-to-all-start.5
  356.4 1.6 copy.86
  360.5 19.6 %all-to-all-done.5 = bf16[16,32,3,512]{3,1,2,0:T(8,128)(2,1)} async-done(((bf16[16,32,3,512]{3,1,2,0:T(8,128)(2,1)}), bf16[16,32,3,512]{3,1,2,0:T(8,128)(2,1)}, u32[]{:S(2)}, u32[]{:S(2)}) %all-to-all-start.5) | async-done | bytes 1572896 | tf_op jit(solution)/shard_map/all_to_all | solution.py:70
  380.1 1.4 stack.133
  381.4 4.4 all-to-all-start.3
  386.1 1.5 copy.90
  387.6 1.6 convolution_bitcast_fusion.3
  394.1 15.4 %all-to-all-done.3 = bf16[16,32,3,512]{3,1,2,0:T(8,128)(2,1)} async-done(((bf16[16,32,3,512]{3,1,2,0:T(8,128)(2,1)}), bf16[16,32,3,512]{3,1,2,0:T(8,128)(2,1)}, u32[]{:S(2)}, u32[]{:S(2)}) %all-to-all-start.3) | async-done | bytes 1572896 | tf_op jit(solution)/shard_map/all_to_all | solution.py:70
  409.5 1.5 copy.82
  417.4 3.5 copy.100
  420.9 1.4 convolution_bitcast_fusion.1
  424.0 3.6 copy.104
  427.6 1.4 convolution_bitcast_fusion.7
  430.7 3.6 copy.96
  436.8 2.2 multiply_reduce_fusion.4
  440.1 2.2 multiply_reduce_fusion.3
  443.5 2.2 multiply_reduce_fusion.5
  446.8 2.2 multiply_reduce_fusion.1
  450.1 2.2 multiply_reduce_fusion
  453.5 1.5 multiply_reduce_fusion.2
  456.6 159.9 %all-reduce.11.cloned.1.call-done = (f32[512,3,512]{2,1,0:T(4,128)}, f32[512,3,512]{2,1,0:T(4,128)}, f32[512,3,512]{2,1,0:T(4,128)}) async-done(((f32[512,3,512]{2,1,0:T(4,128)}, f32[512,3,512]{2,1,0:T(4,128)}, f32[512,3,512]{2,1,0:T(4,128)}), (f32[512,3,512]{2,1,0:T(4,128)}, f32[512,3,512]{2,1,0:T(4,128)}, f32[512,3,512]{2,1,0:T(4,128)})) %all-reduce.11.cloned.1.call-update) | async-done | bytes 9437200
  616.5 1.4 fusion.56
  (194 shorter events, 52.4 us)
Async XLA Ops:
  8.4 39.1 %copy-start.32 = (f32[1,1,32,3,512]{4,2,3,1,0:T(8,128)}, f32[1,1,32,3,512]{4,2,3,1,0:T(8,128)S(1)}, u32[]{:S(2)}) copy-start(f32[1,1,32,3,512]{4,2,3,1,0:T(8,128)S(1)} %get-tuple-element.18) | copy-start | bytes 589828
  10.7 30.7 %all-to-all-start.1 = ((bf16[16,32,3,512]{3,1,2,0:T(8,128)(2,1)}), bf16[16,32,3,512]{3,1,2,0:T(8,128)(2,1)S(1)}, u32[]{:S(2)}, u32[]{:S(2)}) async-start(bf16[16,32,3,512]{3,1,2,0:T(8,128)(2,1)} %stack.110), calls=%async_computation.1 | async-start | bytes 3145728 | tf_op jit(solution)/shard_map/all_to_all | solution.py:70
  41.4 1.7 copy-start.14
  42.9 4.8 copy-start.51
  43.0 28.1 %all-to-all-start.2 = ((bf16[16,32,3,512]{3,1,2,0:T(8,128)(2,1)}), bf16[16,32,3,512]{3,1,2,0:T(8,128)(2,1)}, u32[]{:S(2)}, u32[]{:S(2)}) async-start(bf16[16,32,3,512]{3,1,2,0:T(8,128)(2,1)} %stack.112), calls=%async_computation.2 | async-start | bytes 3145728 | tf_op jit(solution)/shard_map/all_to_all | solution.py:70
  47.7 1.6 copy-start
  49.3 34.5 %copy-start.2 = (bf16[16,32,3,512]{3,1,0,2:T(8,128)(2,1)}, bf16[16,32,3,512]{3,1,0,2:T(8,128)(2,1)S(1)}, u32[]{:S(2)}) copy-start(bf16[16,32,3,512]{3,1,0,2:T(8,128)(2,1)S(1)} %copy.66) | copy-start | bytes 4718596
  72.5 28.1 %all-to-all-start = ((bf16[16,32,3,512]{3,1,2,0:T(8,128)(2,1)}), bf16[16,32,3,512]{3,1,2,0:T(8,128)(2,1)}, u32[]{:S(2)}, u32[]{:S(2)}) async-start(bf16[16,32,3,512]{3,1,2,0:T(8,128)(2,1)} %stack.108), calls=%async_computation | async-start | bytes 3145728 | tf_op jit(solution)/shard_map/all_to_all | solution.py:70
  76.9 230.6 %all-reduce.13.cloned.1.call-start = ((), (), s32[]{:S(2)}) async-start(), calls=%async_computation.7 | async-start | bytes 25165824
  78.5 5.5 copy-start.4
  102.1 2.6 copy-start.6
  102.3 3.3 copy-start.26
  105.6 1.6 copy-start.40
  112.0 2.7 copy-start.19
  115.0 3.6 copy-start.27
  118.6 1.5 copy-start.44
  118.6 2.7 copy-start.22
  125.3 182.3 %copy-start.33 = (f32[1,1,32,3,512]{4,2,3,1,0:T(8,128)S(1)}, f32[1,1,32,3,512]{4,2,3,1,0:T(8,128)}, u32[]{:S(2)}) copy-start(f32[1,1,32,3,512]{4,2,3,1,0:T(8,128)} %copy-done.32) | copy-start | bytes 589828
  125.3 183.4 %copy-start.37 = (f32[1,1,32,3,512]{4,2,3,1,0:T(8,128)S(1)}, f32[1,1,32,3,512]{4,2,3,1,0:T(8,128)}, u32[]{:S(2)}) copy-start(f32[1,1,32,3,512]{4,2,3,1,0:T(8,128)} %copy-done.36) | copy-start | bytes 589828
  125.3 184.5 %copy-start.35 = (f32[1,1,32,3,512]{4,2,3,1,0:T(8,128)S(1)}, f32[1,1,32,3,512]{4,2,3,1,0:T(8,128)}, u32[]{:S(2)}) copy-start(f32[1,1,32,3,512]{4,2,3,1,0:T(8,128)} %copy-done.34) | copy-start | bytes 589828
  125.3 194.4 %copy-start.38 = (f32[3,32,3,512]{3,1,2,0:T(8,128)S(1)}, f32[3,32,3,512]{3,1,2,0:T(8,128)}, u32[]{:S(2)}) copy-start(f32[3,32,3,512]{3,1,2,0:T(8,128)} %param.12) | copy-start | bytes 1769476
  311.1 8.6 %collective-permute-start = (bf16[3,32,3,512]{3,1,2,0:T(8,128)(2,1)S(1)}, bf16[3,32,3,512]{3,1,2,0:T(8,128)(2,1)S(1)}, u32[]{:S(2)}, u32[]{:S(2)}) collective-permute-start(bf16[3,32,3,512]{3,1,2,0:T(8,128)(2,1)S(1)} %pad_maximum_fusion.7), channel_id=1, source_target_pairs={{0,16},{16,32},{32,48},{48,64},{64,80},{80,96},{96,112},{112,128},... | collective-permute-start | bytes 884744 | tf_op jit(solution)/shard_map/ppermute | solution.py:12
  322.7 27.6 %all-to-all-start.4 = ((bf16[16,32,3,512]{3,1,2,0:T(8,128)(2,1)}), bf16[16,32,3,512]{3,1,2,0:T(8,128)(2,1)S(1)}, u32[]{:S(2)}, u32[]{:S(2)}) async-start(bf16[16,32,3,512]{3,1,2,0:T(8,128)(2,1)} %stack.136), calls=%async_computation.4 | async-start | bytes 3145728 | tf_op jit(solution)/shard_map/all_to_all | solution.py:70
  350.3 1.7 copy-start.15
  352.0 28.1 %all-to-all-start.5 = ((bf16[16,32,3,512]{3,1,2,0:T(8,128)(2,1)}), bf16[16,32,3,512]{3,1,2,0:T(8,128)(2,1)}, u32[]{:S(2)}, u32[]{:S(2)}) async-start(bf16[16,32,3,512]{3,1,2,0:T(8,128)(2,1)} %stack.139), calls=%async_computation.5 | async-start | bytes 3145728 | tf_op jit(solution)/shard_map/all_to_all | solution.py:70
  356.4 1.6 copy-start.1
  358.0 34.9 %copy-start.8 = (bf16[16,32,3,512]{3,1,0,2:T(8,128)(2,1)}, bf16[16,32,3,512]{3,1,0,2:T(8,128)(2,1)S(1)}, u32[]{:S(2)}) copy-start(bf16[16,32,3,512]{3,1,0,2:T(8,128)(2,1)S(1)} %copy.86) | copy-start | bytes 4718596
  381.4 28.1 %all-to-all-start.3 = ((bf16[16,32,3,512]{3,1,2,0:T(8,128)(2,1)}), bf16[16,32,3,512]{3,1,2,0:T(8,128)(2,1)}, u32[]{:S(2)}, u32[]{:S(2)}) async-start(bf16[16,32,3,512]{3,1,2,0:T(8,128)(2,1)} %stack.133), calls=%async_computation.3 | async-start | bytes 3145728 | tf_op jit(solution)/shard_map/all_to_all | solution.py:70
  385.8 230.7 %all-reduce.11.cloned.1.call-start = ((), (), s32[]{:S(2)}) async-start(), calls=%async_computation.6 | async-start | bytes 25165824
  387.6 5.6 copy-start.10
  411.0 2.6 copy-start.12
  411.3 3.3 copy-start.24
  414.6 1.6 copy-start.39
  420.9 2.7 copy-start.18
  424.0 3.6 copy-start.25
  427.6 1.5 copy-start.43
  427.6 2.7 copy-start.23
  436.8 2.2 copy-start.5
  440.1 2.2 copy-start.7
  443.5 2.2 copy-start.9
  446.8 2.2 copy-start.11
  450.1 2.2 copy-start.13
  453.5 1.6 copy-start.47
  453.5 1.6 copy-start.49
  453.5 1.7 copy-start.46
  453.5 1.7 copy-start.48
  453.5 1.8 copy-start.45
  455.5 161.0 %copy-start.17 = (f32[3,32,3,512]{3,2,1,0:T(4,128)S(1)}, f32[3,32,3,512]{3,2,1,0:T(4,128)}, u32[]{:S(2)}) copy-start(f32[3,32,3,512]{3,2,1,0:T(4,128)} %copy-done.16) | copy-start | bytes 1769476
  (14 other events, 16.4 us)
Sparse Core Ops, SparseCore 0:
  125.4 182.0 all-reduce.12
  434.4 182.0 all-reduce.10
